TPU v7x, 256 devices: a whole 4x4x8 slice. The times are simulated.
256 devices in a mesh: rows: 64 (over y, x_lo, z), cols: 4 (over x_hi, core).
Axes of the slice: x: 4 (x_hi: 2, x_lo: 2; x = x_hi * 2 + x_lo), y: 4, z: 8, core: 2. Of those that a mesh axis runs over, the one named last changes fastest.
Arguments:
- right_vecs: bfloat16 [2, 131072, 512], P(None, 'rows', 'cols'), may hold values from -6 to 6
- left_vecs: bfloat16 [2, 131072, 512], P(None, 'rows', 'cols'), may hold values from -0.046875 to 0.046875
- dip_blocks: bfloat16 [1024, 8, 2, 128, 128], P('rows'), may hold values from -0.125 to 0.125
- block_cols: int32 [1024, 8], P('rows'), may hold values from 0 to 1023, as said below
- block_counts: int32 [1024], P('rows'), may hold values from 1 to 8, as said below
Outputs:
- coupling: float32 [4, 128, 2, 512], P(None, 'rows')
Inputs may be any that keep to these rules, and one draw needn't show every extreme that they name: Block row r's columns lie within 16 blocks of r: |block_cols[r, j] - r| <= 16, slots at or past block_counts[r] included; such slots are not used. Slots in use fill the first block_counts[r] slots of a block row.
All inputs are finite; a program needn't handle non-finite values.
Results may differ from a plain program's by a relative error of at most 0.0029.
Values may be sent and summed in bfloat16 or wider, within the bound.
No kernel may reach another device: no remote copies, remote signals or barrier semaphores. Data moves between devices by JAX's collectives and lax.ppermute only.
A program may use at most 128 MiB of HBM per device.

v0:
```python
import jax
import jax.numpy as jnp
from jax import lax
from jax.sharding import PartitionSpec as P


def padded(block, sides, width):
    for axis, dim in sides:
        count = lax.axis_size(axis)
        forward = [(i, i + 1) for i in range(count - 1)]
        backward = [(target, source) for source, target in forward]
        low = lax.ppermute(
            lax.slice_in_dim(block, block.shape[dim] - width, None, axis=dim), axis, forward
        )
        high = lax.ppermute(lax.slice_in_dim(block, 0, width, axis=dim), axis, backward)
        block = jnp.concatenate([low, block, high], axis=dim)
    return block


def inner_rows(first, second):
    return lax.dot_general(
        first, second, (((0,), (0,)), ((), ())), preferred_element_type=jnp.float32
    )


def project(left, right):
    real_part = inner_rows(left[0], right[0]) + inner_rows(left[1], right[1])
    imag_part = inner_rows(left[0], right[1]) - inner_rows(left[1], right[0])
    return jnp.stack([real_part, imag_part], axis=1)


def apply_blocks(mats, vecs):
    return jnp.einsum("ijpq,ijqk->ipk", mats, vecs, preferred_element_type=jnp.float32)


def local(right_vecs, left_vecs, dip_blocks, block_cols, block_counts):
    span = right_vecs.shape[1]
    width = right_vecs.shape[2]
    blocks_dev = dip_blocks.shape[0]
    slots = dip_blocks.shape[1]
    block_size = dip_blocks.shape[3]
    extended = padded(right_vecs, (("rows", 1),), span)
    stacked = extended.reshape(2, 3 * blocks_dev, block_size, width)
    first_block = (lax.axis_index("rows") - 1) * blocks_dev
    local_cols = block_cols - first_block
    picked = jnp.take(stacked, local_cols.reshape(-1), axis=1).reshape(
        2, blocks_dev, slots, block_size, width
    )
    valid = lax.broadcasted_iota(jnp.int32, (blocks_dev, slots), 1) < block_counts[:, None]
    picked = jnp.where(valid[None, :, :, None, None], picked, jnp.zeros_like(picked))
    dip_real = dip_blocks[:, :, 0]
    dip_imag = dip_blocks[:, :, 1]
    image_real = apply_blocks(dip_real, picked[0]) - apply_blocks(dip_imag, picked[1])
    image_imag = apply_blocks(dip_real, picked[1]) + apply_blocks(dip_imag, picked[0])
    image = jnp.stack([image_real, image_imag]).reshape(2, span, width).astype(jnp.bfloat16)
    partial_value = project(left_vecs, lax.all_gather(image, "cols", axis=2, tiled=True))
    shares = lax.psum_scatter(partial_value, "rows", scatter_dimension=0, tiled=True)
    return lax.all_gather(shares[None], "cols", axis=0, tiled=True)


def solution(mesh):
    in_specs = (
        P(None, "rows", "cols"),
        P(None, "rows", "cols"),
        P("rows", None, None, None, None),
        P("rows", None),
        P("rows"),
    )
    out_specs = P(None, "rows", None, None)
    return jax.shard_map(local, mesh=mesh, in_specs=in_specs, out_specs=out_specs, check_vma=False)
```

profile of v0, /device:TPU:1, one launch (start us, length us, event | category | flops | bytes accessed | tf_op | source)
XLA Modules:
  0.0 743.3 jit_solution(18084673768489570495)
XLA Ops:
  6.5 4.4 collective-permute-start
  11.0 1.3 collective-permute-start.1
  13.2 0.7 iota_compare_fusion
  14.0 19.1 %collective-permute-done = bf16[2,2048,128]{2,1,0:T(8,128)(2,1)S(1)} collective-permute-done((bf16[2,2048,128]{2,1,0:T(8,128)(2,1)}, bf16[2,2048,128]{2,1,0:T(8,128)(2,1)S(1)}, u32[]{:S(2)}, u32[]{:S(2)}) %collective-permute-start) | collective-permute-done | bytes 1048608 | tf_op jit(solution)/shard_map/ppermute | solution.py:12
  33.0 1.0 copy-done
  34.0 3.1 collective-permute-done.1
  37.2 2.0 pad_maximum_fusion
  39.1 6.5 gather_fusion
  45.7 10.5 %copy.19 = bf16[2,128,128,128]{3,2,1,0:T(8,128)(2,1)} copy(bf16[2,128,128,128]{3,2,0,1:T(8,128)(2,1)} %bitcast.123) | data formatting | bytes 16777216 | tf_op jit(solution)/shard_map/jit(_take)/gather | solution.py:46
  56.2 5.0 select_select_fusion
  61.2 1.2 fusion.19
  62.4 1.2 fusion.16
  63.7 1.3 fusion.37
  65.0 1.3 fusion.34
  66.2 1.1 pad_maximum_fusion.1
  67.6 45.6 %all-gather.3.cloned.1.call-done = bf16[2,2048,512]{2,1,0:T(8,128)(2,1)} async-done(((bf16[2,2048,128]{2,1,0:T(8,128)(2,1)}), bf16[2,2048,512]{2,1,0:T(8,128)(2,1)}) %all-gather.3.cloned.1.call-update) | async-done | bytes 4194320 | tf_op jit(solution)/shard_map/all_gather | solution.py:56
  113.2 2.5 fusion.13
  116.0 0.7 fusion.12
  116.7 0.8 fusion.41
  117.5 0.7 fusion.43
  118.3 1.0 copy.22
  120.6 561.3 %all-reduce.3.cloned.1.call-done = f32[128,2,512]{2,1,0:T(2,128)} async-done(((f32[128,2,512]{2,1,0:T(2,128)}), f32[128,2,512]{2,1,0:T(2,128)}) %all-reduce.3.cloned.1.call-update) | async-done | bytes 524304
  681.9 0.7 constant_dynamic-slice_fusion
  682.6 53.2 %all-gather = f32[8,2,512]{2,1,0:T(2,128)S(1)} all-gather(f32[2,2,512]{2,1,0:T(2,128)S(1)} %constant_dynamic-slice_fusion), channel_id=2, replica_groups=mesh['rows'=64,'cols'=4] {'cols'}, dimensions={0}, use_global_device_ids=true | all-gather | bytes 40960 | tf_op jit(solution)/shard_map/all_gather | solution.py:58
  (25 shorter events, 2.8 us)
Async XLA Ops:
  6.5 106.6 %all-gather.3.cloned.1.call-start = ((), (), s32[]{:S(2)}) async-start(), calls=%async_computation | async-start | bytes 5242880 | tf_op jit(solution)/shard_map/all_gather | solution.py:56
  6.5 26.5 %collective-permute-start = (bf16[2,2048,128]{2,1,0:T(8,128)(2,1)}, bf16[2,2048,128]{2,1,0:T(8,128)(2,1)S(1)}, u32[]{:S(2)}, u32[]{:S(2)}) collective-permute-start(bf16[2,2048,128]{2,1,0:T(8,128)(2,1)} %param.5), channel_id=1, source_target_pairs={{0,4},{4,8},{8,12},{12,16},{16,20},{20,24},{24,28},{28,32},{32,36}... | collective-permute-start | bytes 3145736 | tf_op jit(solution)/shard_map/ppermute | solution.py:12
  11.0 26.2 %collective-permute-start.1 = (bf16[2,2048,128]{2,1,0:T(8,128)(2,1)}, bf16[2,2048,128]{2,1,0:T(8,128)(2,1)}, u32[]{:S(2)}, u32[]{:S(2)}) collective-permute-start(bf16[2,2048,128]{2,1,0:T(8,128)(2,1)} %param.5), channel_id=1, source_target_pairs={{4,0},{8,4},{12,8},{16,12},{20,16},{24,20},{28,24},{32,28},{36,32}... | collective-permute-start | bytes 3145736 | tf_op jit(solution)/shard_map/ppermute | solution.py:15
  33.0 1.0 copy-start
  45.7 15.5 %slice-start = ((s8[8388608]{0:T(1024)(128)(4,1)}), s8[4194304]{0:T(1024)(128)(4,1)S(1)}, s32[]{:S(2)}) async-start(s8[8388608]{0:T(1024)(128)(4,1)} %bitcast.127), calls=%async_computation.2 | async-start | bytes 8388608
  56.2 5.0 slice-start.1
  65.0 48.2 %copy-start.2 = (bf16[2,2048,128]{2,1,0:T(8,128)(2,1)S(1)}, bf16[2,2048,128]{2,1,0:T(8,128)(2,1)}, u32[]{:S(2)}) copy-start(bf16[2,2048,128]{2,1,0:T(8,128)(2,1)} %param.6) | copy-start | bytes 3145732
  67.3 614.6 %all-reduce.3.cloned.1.call-start = ((), (), s32[]{:S(2)}) async-start(), calls=%async_computation.1 | async-start | bytes 1048576
  113.2 2.8 copy-start.1
  117.5 1.8 copy-start.3
Sparse Core Ops, SparseCore 0:
  67.4 45.6 all-gather.2
  119.4 562.4 all-reduce.2
where the time goes:
time: 744 us; the launch traced here: 743 us
  waiting for transfers between devices  629 us (85%)
  blocking collectives  53.2 us (7%)
  local copies, waits for them, and re-layouts  21.6 us (3%)
  between operations  14.2 us (2%)
  matrix products  9.72 us (1%)
  other arithmetic  9.46 us (1%)
    unnamed x3, waiting for transfers between devices  561 us
    all_gather x1, blocking collectives, local(): return lax.all_gather(shares[None], 'cols', axis=0, tiled=True)  53.2 us
    all_gather x1, waiting for transfers between devices, local(): lax.all_gather(image, 'cols', axis=2, tiled=True)  45.6 us
    ppermute x1, waiting for transfers between devices, padded(): lax.ppermute(lax.slice_in_dim(block, block.shape[dim] - width, None, axis...  19.1 us
    gather x2, local copies, waits for them, and re-layouts, local(): jnp.take(stacked, local_cols.reshape(-1), axis=1)  17.1 us
  transfers between devices with their start and end apart: 4, of which 4 were waited for; matrix products, arithmetic and copies ran while one was open for 0% of the time, Pallas kernels for 0%

commit v1 on v0

v1 whole, which is shorter than its diff:
```python
import jax
import jax.numpy as jnp
from jax import lax
from jax.experimental import pallas as pl
from jax.experimental.pallas import tpu as pltpu
from jax.sharding import PartitionSpec as P


ROWS_STEP = 2


def whole(shape):
    return pl.BlockSpec(shape, lambda i, *_: (0,) * len(shape))


def params(mib):
    return pltpu.CompilerParams(dimension_semantics=("arbitrary",), vmem_limit_bytes=mib * 1024 * 1024)


def build_weights(weights, ref, base):
    _, blocks, size, width = ref.shape

    def build(i, carry):
        real = ref[0, i]
        imag = ref[1, i]
        weights[base + i, :size, :width] = real
        weights[base + i, :size, width:] = imag
        weights[base + i, size:, :width] = -imag
        weights[base + i, size:, width:] = real
        return carry

    lax.fori_loop(0, blocks, build, 0)


def add_slots(acc, k, row, cols_ref, counts_ref, dip_ref, weights, pick):
    def slot(j, carry):
        used, at = pick(cols_ref[row, j])

        @pl.when(used)
        def _():
            lhs = jnp.concatenate([dip_ref[k, j, 0], dip_ref[k, j, 1]], axis=1)
            acc[k] += jnp.dot(lhs, weights[at], preferred_element_type=jnp.float32)

        return carry

    lax.fori_loop(0, counts_ref[row], slot, 0)


def own_kernel(cols_ref, counts_ref, own_ref, dip_ref, acc_ref, weights):
    step = pl.program_id(0)
    blocks = own_ref.shape[1]

    @pl.when(step == 0)
    def _():
        build_weights(weights, own_ref, 0)

    def pick(col):
        return (col >= blocks) & (col < 2 * blocks), col - blocks

    acc_ref[...] = jnp.zeros_like(acc_ref)
    for k in range(ROWS_STEP):
        add_slots(acc_ref, k, step * ROWS_STEP + k, cols_ref, counts_ref, dip_ref, weights, pick)


def halo_kernel(cols_ref, counts_ref, low_ref, high_ref, dip_ref, acc_in_ref, image_ref, weights, acc):
    step = pl.program_id(0)
    blocks = low_ref.shape[1]

    @pl.when(step == 0)
    def _():
        build_weights(weights, low_ref, 0)
        build_weights(weights, high_ref, blocks)

    def pick(col):
        return (col < blocks) | (col >= 2 * blocks), jnp.where(col < blocks, col, col - blocks)

    acc[...] = acc_in_ref[...]
    for k in range(ROWS_STEP):
        add_slots(acc, k, step * ROWS_STEP + k, cols_ref, counts_ref, dip_ref, weights, pick)
    image_ref[...] = acc[...].astype(image_ref.dtype)


def specs(dips, width):
    _, slots, _, size, _ = dips.shape
    dip = pl.BlockSpec((ROWS_STEP, slots, 2, size, size), lambda i, *_: (i, 0, 0, 0, 0))
    acc = pl.BlockSpec((ROWS_STEP, size, 2 * width), lambda i, *_: (i, 0, 0))
    return dip, acc


def own_products(cols, counts, own, dips):
    rows, _, _, size, _ = dips.shape
    width = own.shape[-1]
    dip, acc = specs(dips, width)
    return pl.pallas_call(
        own_kernel,
        out_shape=jax.ShapeDtypeStruct((rows, size, 2 * width), jnp.float32),
        grid_spec=pltpu.PrefetchScalarGridSpec(
            num_scalar_prefetch=2,
            grid=(rows // ROWS_STEP,),
            in_specs=[whole(own.shape), dip],
            out_specs=acc,
            scratch_shapes=[pltpu.VMEM((rows, 2 * size, 2 * width), jnp.bfloat16)],
        ),
        compiler_params=params(16),
        cost_estimate=pl.CostEstimate(flops=1_000_000_000, bytes_accessed=11_000_000, transcendentals=0),
    )(cols, counts, own, dips)


def halo_products(cols, counts, low, high, dips, acc_in):
    rows, _, _, size, _ = dips.shape
    width = low.shape[-1]
    dip, acc = specs(dips, width)
    return pl.pallas_call(
        halo_kernel,
        out_shape=jax.ShapeDtypeStruct((rows, size, 2 * width), jnp.bfloat16),
        grid_spec=pltpu.PrefetchScalarGridSpec(
            num_scalar_prefetch=2,
            grid=(rows // ROWS_STEP,),
            in_specs=[whole(low.shape), whole(high.shape), dip, acc],
            out_specs=acc,
            scratch_shapes=[
                pltpu.VMEM((2 * rows, 2 * size, 2 * width), jnp.bfloat16),
                pltpu.VMEM((ROWS_STEP, size, 2 * width), jnp.float32),
            ],
        ),
        compiler_params=params(24),
        cost_estimate=pl.CostEstimate(flops=1_000_000_000, bytes_accessed=12_000_000, transcendentals=0),
    )(cols, counts, low, high, dips, acc_in)


def project_kernel(left_ref, image_ref, other_ref, out_ref, total):
    step = pl.program_id(0)
    width = left_ref.shape[-1]
    chunks, each2, _ = out_ref.shape
    each = each2 // 2

    @pl.when(step == 0)
    def _():
        total[...] = jnp.zeros_like(total)

    images = jnp.concatenate([image_ref[...], other_ref[...]], axis=1)
    for part in range(2):
        total[part] += lax.dot_general(
            left_ref[part], images, (((0,), (0,)), ((), ())), preferred_element_type=jnp.float32
        )

    @pl.when(step == pl.num_programs(0) - 1)
    def _():
        for t in range(2):
            re = slice(2 * t * width, (2 * t + 1) * width)
            im = slice((2 * t + 1) * width, (2 * t + 2) * width)
            to = slice(t * width, (t + 1) * width)
            real = total[0, :, re] + total[1, :, im]
            imag = total[0, :, im] - total[1, :, re]
            out_ref[:, :each, to] = real.reshape(chunks, each, width)
            out_ref[:, each:, to] = imag.reshape(chunks, each, width)


def project(left, image, other, chunks):
    _, span, width = left.shape
    each = width // chunks
    tile = min(512, span)
    return pl.pallas_call(
        project_kernel,
        out_shape=jax.ShapeDtypeStruct((chunks, 2 * each, 2 * width), jnp.float32),
        grid_spec=pl.GridSpec(
            grid=(span // tile,),
            in_specs=[
                pl.BlockSpec((2, tile, width), lambda i: (0, i, 0)),
                pl.BlockSpec((tile, 2 * width), lambda i: (i, 0)),
                pl.BlockSpec((tile, 2 * width), lambda i: (i, 0)),
            ],
            out_specs=whole((chunks, 2 * each, 2 * width)),
            scratch_shapes=[pltpu.VMEM((2, width, 4 * width), jnp.float32)],
        ),
        compiler_params=params(16),
        cost_estimate=pl.CostEstimate(flops=600_000_000, bytes_accessed=3_500_000, transcendentals=0),
    )(left, image, other)


def local(right_vecs, left_vecs, dip_blocks, block_cols, block_counts):
    parts, span, width = right_vecs.shape
    blocks, _, _, size, _ = dip_blocks.shape
    n_rows = lax.axis_size("rows")
    n_cols = lax.axis_size("cols")
    each = width // n_rows
    forward = [(i, i + 1) for i in range(n_rows - 1)]
    backward = [(j, i) for i, j in forward]
    blocked = lambda x: x.reshape(parts, blocks, size, width)
    local_cols = block_cols - (lax.axis_index("rows") - 1) * blocks
    low = lax.ppermute(right_vecs, "rows", forward)
    high = lax.ppermute(right_vecs, "rows", backward)
    across = lax.ppermute(left_vecs, "cols", [(i, i ^ 2) for i in range(n_cols)])
    acc = own_products(local_cols, block_counts, blocked(right_vecs), dip_blocks)
    image = halo_products(local_cols, block_counts, blocked(low), blocked(high), dip_blocks, acc)
    image = image.reshape(span, 2 * width)
    other = lax.ppermute(image, "cols", [(i, i ^ 1) for i in range(n_cols)])
    near = project(left_vecs, image, other, n_rows)
    far = project(across, image, other, n_rows)
    partial = jnp.concatenate([near, far], axis=1).astype(jnp.bfloat16)
    received = lax.all_to_all(partial, "rows", 0, 0, tiled=True)
    share = jnp.sum(received.astype(jnp.float32), axis=0).reshape(2, parts, each, 2, width)
    me = lax.axis_index("cols")
    share = jnp.where((me & 2) > 0, share[::-1], share)
    share = jnp.where((me & 1) > 0, share[:, :, :, ::-1], share)
    out = lax.all_gather(share.reshape(2 * parts * each, 2 * width), "cols", axis=0)
    out = out.reshape(2, 2, 2, parts, each, 2, width)
    return out.transpose(2, 1, 4, 3, 0, 5, 6).reshape(n_cols, each, parts, n_cols * width)


def solution(mesh):
    in_specs = (
        P(None, "rows", "cols"),
        P(None, "rows", "cols"),
        P("rows", None, None, None, None),
        P("rows", None),
        P("rows"),
    )
    out_specs = P(None, "rows", None, None)
    return jax.shard_map(local, mesh=mesh, in_specs=in_specs, out_specs=out_specs, check_vma=False)
```

time: 744 us -> 107 us (0.14)
  waiting for transfers between devices: 629 us -> 47.1 us
  blocking collectives: 53.2 us -> 9.65 us
  starting transfers between devices: 5.93 us -> 30.1 us
  local copies, waits for them, and re-layouts: 21.6 us -> 6.77 us
  between operations: 14.2 us -> 0.14 us
  Pallas kernels: 0 us -> 11.5 us
  matrix products: 9.72 us -> 0 us
  other arithmetic: 9.46 us -> 1.02 us
    unnamed x3 -> x0, waiting for transfers between devices: 561 us -> none
    all_gather x1 -> x0, waiting for transfers between devices: 45.6 us -> none  [local(): lax.all_gather(image, 'cols', axis=2, tiled=True)]
    all_gather x1, blocking collectives: 53.2 us -> 9.65 us  [local(): lax.all_gather(share.reshape(2 * parts * each, 2 * width), 'cols', axis=0)]
    all_to_all x0 -> x1, starting transfers between devices: none -> 19.8 us  [local(): received = lax.all_to_all(partial, 'rows', 0, 0, tiled=True)]
    gather x2 -> x0, local copies, waits for them, and re-layouts: 17.1 us -> none  [local(): jnp.take(stacked, local_cols.reshape(-1), axis=1)]
    ppermute x2 -> x4, waiting for transfers between devices: 22.2 us -> 35.7 us  [the longest x1 21.7 us: local(): lax.ppermute(left_vecs, 'cols', [(i, i ^ 2) for i in range(n_cols)])]
    pallas_call x0 -> x4, Pallas kernels: none -> 11.5 us  [the longest x1 4.71 us: own_products(): pl.pallas_call(own_kernel, out_shape=jax.ShapeDtypeStruct((rows, size, 2...]
    all_to_all x0 -> x1, waiting for transfers between devices: none -> 11.4 us  [local(): received = lax.all_to_all(partial, 'rows', 0, 0, tiled=True)]
  transfers between devices with their start and end apart: 4 -> 5, of which waited for: 4 -> 4; matrix products, arithmetic and copies ran while one was open for 0% -> 1% of each run, Pallas kernels for 0% -> 6%
where the time goes in v1:
time: 107 us; the launch traced here: 106 us
  waiting for transfers between devices  47.1 us (44%)
  starting transfers between devices  30.1 us (28%)
  Pallas kernels  11.5 us (11%)
  blocking collectives  9.65 us (9%)
  local copies, waits for them, and re-layouts  6.77 us (6%)
    ppermute x1, waiting for transfers between devices, local(): lax.ppermute(left_vecs, 'cols', [(i, i ^ 2) for i in range(n_cols)])  21.7 us
    all_to_all x1, starting transfers between devices, local(): received = lax.all_to_all(partial, 'rows', 0, 0, tiled=True)  19.8 us
    all_to_all x1, waiting for transfers between devices, local(): received = lax.all_to_all(partial, 'rows', 0, 0, tiled=True)  11.4 us
    ppermute x1, waiting for transfers between devices, local(): low = lax.ppermute(right_vecs, 'rows', forward)  10 us
    all_gather x1, blocking collectives, local(): lax.all_gather(share.reshape(2 * parts * each, 2 * width), 'cols', axis=0)  9.65 us
    unnamed x13, local copies, waits for them, and re-layouts  6.03 us
    pallas_call x1, Pallas kernels, own_products(): pl.pallas_call(own_kernel, out_shape=jax.ShapeDtypeStruct((rows, size, 2...  4.71 us
    ppermute x1, starting transfers between devices, local(): low = lax.ppermute(right_vecs, 'rows', forward)  4.55 us
  transfers between devices with their start and end apart: 5, of which 4 were waited for; matrix products, arithmetic and copies ran while one was open for 1% of the time, Pallas kernels for 6%

profile of v1, /device:TPU:1, one launch (start us, length us, event | category | flops | bytes accessed | tf_op | source)
XLA Modules:
  0.0 106.3 jit_solution(10070101968433927149)
XLA Ops:
  0.0 4.5 %collective-permute-start = (bf16[2,2048,128]{2,1,0:T(8,128)(2,1)}, bf16[2,2048,128]{2,1,0:T(8,128)(2,1)S(1)}, u32[]{:S(2)}, u32[]{:S(2)}) collective-permute-start(bf16[2,2048,128]{2,1,0:T(8,128)(2,1)} %param.5), channel_id=1, source_target_pairs={{0,4},{4,8},{8,12},{12,16},{16,20},{20,24},{24,28},{28,32},{32,36}... | collective-permute-start | bytes 3145736 | tf_op jit(solution)/shard_map/ppermute | solution.py:191
  4.6 1.3 %collective-permute-start.1 = (bf16[2,2048,128]{2,1,0:T(8,128)(2,1)}, bf16[2,2048,128]{2,1,0:T(8,128)(2,1)S(1)}, u32[]{:S(2)}, u32[]{:S(2)}) collective-permute-start(bf16[2,2048,128]{2,1,0:T(8,128)(2,1)} %param.5), channel_id=1, source_target_pairs={{4,0},{8,4},{12,8},{16,12},{20,16},{24,20},{28,24},{32,28},{36,32}... | collective-permute-start | bytes 3145736 | tf_op jit(solution)/shard_map/ppermute | solution.py:192
  5.9 0.8 copy.10
  6.6 3.4 %copy-done = bf16[16,8,2,128,128]{4,3,2,1,0:T(8,128)(2,1)S(1)} copy-done((bf16[16,8,2,128,128]{4,3,2,1,0:T(8,128)(2,1)S(1)}, bf16[16,8,2,128,128]{4,3,2,1,0:T(8,128)(2,1)}, u32[]{:S(2)}) %copy-start) | copy-done | bytes 8388632
  10.0 1.2 %copy-done.2 = bf16[2,2048,128]{2,1,0:T(8,128)(2,1)S(1)} copy-done((bf16[2,2048,128]{2,1,0:T(8,128)(2,1)S(1)}, bf16[2,2048,128]{2,1,0:T(8,128)(2,1)}, u32[]{:S(2)}) %copy-start.2) | copy-done | bytes 1048600
  11.2 0.7 copy-done.4
  11.9 4.7 %shard_map.55.acc_in_ref = f32[16,128,256]{2,1,0:T(8,128)S(1)} custom-call(s32[16,8]{1,0:T(8,128)S(1)} %broadcast_subtract_fusion.cols_ref, s32[16]{0:T(128)S(1)} %copy-done.4, bf16[2,16,128,128]{3,2,1,0:T(8,128)(2,1)S(1)} %bitcast.8, bf16[16,8,2,128,128]{4,3,2,1,0:T(8,128)(2,1)S(1)} %copy-done), custom_call_target="tpu_custom_call" | custom-call | flops 1000000000 | bytes 11000000 | tf_op jit(solution)/shard_map/pallas_call | solution.py:94
  16.6 0.0 copy-start.3
  16.6 10.0 %collective-permute-done = bf16[2,2048,128]{2,1,0:T(8,128)(2,1)S(1)} collective-permute-done((bf16[2,2048,128]{2,1,0:T(8,128)(2,1)}, bf16[2,2048,128]{2,1,0:T(8,128)(2,1)S(1)}, u32[]{:S(2)}, u32[]{:S(2)}) %collective-permute-start) | collective-permute-done | bytes 1048608 | tf_op jit(solution)/shard_map/ppermute | solution.py:191
  26.6 4.0 %collective-permute-done.1 = bf16[2,2048,128]{2,1,0:T(8,128)(2,1)S(1)} collective-permute-done((bf16[2,2048,128]{2,1,0:T(8,128)(2,1)}, bf16[2,2048,128]{2,1,0:T(8,128)(2,1)S(1)}, u32[]{:S(2)}, u32[]{:S(2)}) %collective-permute-start.1) | collective-permute-done | bytes 1048608 | tf_op jit(solution)/shard_map/ppermute | solution.py:192
  30.7 0.0 copy-done.5
  30.7 3.5 %shard_map.56 = bf16[16,128,256]{2,1,0:T(8,128)(2,1)S(1)} custom-call(s32[16,8]{1,0:T(8,128)S(1)} %broadcast_subtract_fusion.cols_ref, s32[16]{0:T(128)S(1)} %copy-done.5, bf16[2,16,128,128]{3,2,1,0:T(8,128)(2,1)S(1)} %bitcast.9, bf16[2,16,128,128]{3,2,1,0:T(8,128)(2,1)S(1)} %bitcast.10, bf16[16,8,2,128,128]{4,3,2,1,0:T(8,128)(2,1)S(1)} %copy-done.1, ...), custom_call_target="tpu_custom_call" | custom-call | flops 1000000000 | bytes 12000000 | tf_op jit(solution)/shard_map/pallas_call | solution.py:113
  34.2 1.8 %collective-permute-start.2 = (bf16[2048,256]{1,0:T(8,128)(2,1)S(1)}, bf16[2048,256]{1,0:T(8,128)(2,1)S(1)}, u32[]{:S(2)}, u32[]{:S(2)}) collective-permute-start(bf16[2048,256]{1,0:T(8,128)(2,1)S(1)} %bitcast.5), channel_id=1, source_target_pairs={{0,1},{1,0},{2,3},{3,2},{4,5},{5,4},{6,7},{7,6},{8,9},{9,8},{10,11... | collective-permute-start | bytes 3145736 | tf_op jit(solution)/shard_map/ppermute | solution.py:197
  36.0 2.7 %collective-permute-start.3 = (bf16[2,2048,128]{2,1,0:T(8,128)(2,1)S(1)}, bf16[2,2048,128]{2,1,0:T(8,128)(2,1)S(1)}, u32[]{:S(2)}, u32[]{:S(2)}) collective-permute-start(bf16[2,2048,128]{2,1,0:T(8,128)(2,1)S(1)} %copy-done.3), channel_id=1, source_target_pairs={{0,2},{1,3},{2,0},{3,1},{4,6},{5,7},{6,4},{7,5},{8,10},{9,11},{10,... | collective-permute-start | bytes 3145736 | tf_op jit(solution)/shard_map/ppermute | solution.py:193
  38.7 0.0 collective-permute-done.2.other_ref
  38.7 1.6 %shard_map.57 = f32[64,4,256]{2,1,0:T(4,128)S(1)} custom-call(bf16[2,2048,128]{2,1,0:T(8,128)(2,1)S(1)} %copy-done.3, bf16[2048,256]{1,0:T(8,128)(2,1)S(1)} %bitcast.6, bf16[2048,256]{1,0:T(8,128)(2,1)S(1)} %collective-permute-done.2.other_ref), custom_call_target="tpu_custom_call" | custom-call | flops 600000000 | bytes 3500000 | tf_op jit(solution)/shard_map/pallas_call | solution.py:163
  40.4 21.7 %collective-permute-done.3.left_ref = bf16[2,2048,128]{2,1,0:T(8,128)(2,1)S(1)} collective-permute-done((bf16[2,2048,128]{2,1,0:T(8,128)(2,1)S(1)}, bf16[2,2048,128]{2,1,0:T(8,128)(2,1)S(1)}, u32[]{:S(2)}, u32[]{:S(2)}) %collective-permute-start.3) | collective-permute-done | bytes 1048608 | tf_op jit(solution)/shard_map/ppermute | solution.py:193
  62.1 1.6 %shard_map.58 = f32[64,4,256]{2,1,0:T(4,128)S(1)} custom-call(bf16[2,2048,128]{2,1,0:T(8,128)(2,1)S(1)} %collective-permute-done.3.left_ref, bf16[2048,256]{1,0:T(8,128)(2,1)S(1)} %bitcast.7, bf16[2048,256]{1,0:T(8,128)(2,1)S(1)} %collective-permute-done.2.other_ref), custom_call_target="tpu_custom_call" | custom-call | flops 600000000 | bytes 3500000 | tf_op jit(solution)/shard_map/pallas_call | solution.py:163
  63.8 0.8 pad_maximum_fusion
  64.6 19.8 %all-to-all-start = ((bf16[64,8,256]{2,1,0:T(8,128)(2,1)}), bf16[64,8,256]{2,1,0:T(8,128)(2,1)S(1)}, u32[]{:S(2)}, u32[]{:S(2)}) async-start(bf16[64,8,256]{2,1,0:T(8,128)(2,1)} %pad_maximum_fusion), calls=%async_computation | async-start | bytes 524288 | tf_op jit(solution)/shard_map/all_to_all | solution.py:201
  84.4 11.4 %all-to-all-done = bf16[64,8,256]{2,1,0:T(8,128)(2,1)S(1)} async-done(((bf16[64,8,256]{2,1,0:T(8,128)(2,1)}), bf16[64,8,256]{2,1,0:T(8,128)(2,1)S(1)}, u32[]{:S(2)}, u32[]{:S(2)}) %all-to-all-start) | async-done | bytes 262176 | tf_op jit(solution)/shard_map/all_to_all | solution.py:201
  95.8 0.1 convert_reduce_fusion
  95.9 9.7 %all_gather.3 = f32[4,8,256]{2,1,0:T(8,128)S(1)} all-gather(f32[1,8,256]{2,1,0:T(8,128)S(1)} %all_gather_reshape.3), channel_id=1, replica_groups=mesh['rows'=64,'cols'=4] {'cols'}, dimensions={0}, use_global_device_ids=true | all-gather | bytes 40960 | tf_op jit(solution)/shard_map/all_gather | solution.py:206
  105.6 0.7 reshape.27
  (17 shorter events, 0.2 us)
Async XLA Ops:
  0.0 30.7 %copy-start.5 = (s32[16]{0:T(128)S(1)}, s32[16]{0:T(128)}, u32[]{:S(2)}) copy-start(s32[16]{0:T(128)} %counts_ref.3) | copy-start | bytes 196
  0.0 26.6 %collective-permute-start = (bf16[2,2048,128]{2,1,0:T(8,128)(2,1)}, bf16[2,2048,128]{2,1,0:T(8,128)(2,1)S(1)}, u32[]{:S(2)}, u32[]{:S(2)}) collective-permute-start(bf16[2,2048,128]{2,1,0:T(8,128)(2,1)} %param.5), channel_id=1, source_target_pairs={{0,4},{4,8},{8,12},{12,16},{16,20},{20,24},{24,28},{28,32},{32,36}... | collective-permute-start | bytes 3145736 | tf_op jit(solution)/shard_map/ppermute | solution.py:191
  4.6 26.1 %collective-permute-start.1 = (bf16[2,2048,128]{2,1,0:T(8,128)(2,1)}, bf16[2,2048,128]{2,1,0:T(8,128)(2,1)S(1)}, u32[]{:S(2)}, u32[]{:S(2)}) collective-permute-start(bf16[2,2048,128]{2,1,0:T(8,128)(2,1)} %param.5), channel_id=1, source_target_pairs={{4,0},{8,4},{12,8},{16,12},{20,16},{24,20},{28,24},{32,28},{36,32}... | collective-permute-start | bytes 3145736 | tf_op jit(solution)/shard_map/ppermute | solution.py:192
  6.6 3.4 %copy-start = (bf16[16,8,2,128,128]{4,3,2,1,0:T(8,128)(2,1)S(1)}, bf16[16,8,2,128,128]{4,3,2,1,0:T(8,128)(2,1)}, u32[]{:S(2)}) copy-start(bf16[16,8,2,128,128]{4,3,2,1,0:T(8,128)(2,1)} %dip_ref.3) | copy-start | bytes 25165828
  10.0 1.2 %copy-start.2 = (bf16[2,2048,128]{2,1,0:T(8,128)(2,1)S(1)}, bf16[2,2048,128]{2,1,0:T(8,128)(2,1)}, u32[]{:S(2)}) copy-start(bf16[2,2048,128]{2,1,0:T(8,128)(2,1)} %param.5) | copy-start | bytes 3145732
  11.2 0.7 copy-start.4
  11.9 18.8 %copy-start.1 = (bf16[16,8,2,128,128]{4,3,2,1,0:T(8,128)(2,1)S(1)}, bf16[16,8,2,128,128]{4,3,2,1,0:T(8,128)(2,1)}, u32[]{:S(2)}) copy-start(bf16[16,8,2,128,128]{4,3,2,1,0:T(8,128)(2,1)} %dip_ref.3) | copy-start | bytes 25165828
  16.6 19.3 %copy-start.3 = (bf16[2,2048,128]{2,1,0:T(8,128)(2,1)S(1)}, bf16[2,2048,128]{2,1,0:T(8,128)(2,1)}, u32[]{:S(2)}) copy-start(bf16[2,2048,128]{2,1,0:T(8,128)(2,1)} %left_ref.1) | copy-start | bytes 3145732
  34.2 4.5 %collective-permute-start.2 = (bf16[2048,256]{1,0:T(8,128)(2,1)S(1)}, bf16[2048,256]{1,0:T(8,128)(2,1)S(1)}, u32[]{:S(2)}, u32[]{:S(2)}) collective-permute-start(bf16[2048,256]{1,0:T(8,128)(2,1)S(1)} %bitcast.5), channel_id=1, source_target_pairs={{0,1},{1,0},{2,3},{3,2},{4,5},{5,4},{6,7},{7,6},{8,9},{9,8},{10,11... | collective-permute-start | bytes 3145736 | tf_op jit(solution)/shard_map/ppermute | solution.py:197
  36.0 26.1 %collective-permute-start.3 = (bf16[2,2048,128]{2,1,0:T(8,128)(2,1)S(1)}, bf16[2,2048,128]{2,1,0:T(8,128)(2,1)S(1)}, u32[]{:S(2)}, u32[]{:S(2)}) collective-permute-start(bf16[2,2048,128]{2,1,0:T(8,128)(2,1)S(1)} %copy-done.3), channel_id=1, source_target_pairs={{0,2},{1,3},{2,0},{3,1},{4,6},{5,7},{6,4},{7,5},{8,10},{9,11},{10,... | collective-permute-start | bytes 3145736 | tf_op jit(solution)/shard_map/ppermute | solution.py:193
  64.6 31.2 %all-to-all-start = ((bf16[64,8,256]{2,1,0:T(8,128)(2,1)}), bf16[64,8,256]{2,1,0:T(8,128)(2,1)S(1)}, u32[]{:S(2)}, u32[]{:S(2)}) async-start(bf16[64,8,256]{2,1,0:T(8,128)(2,1)} %pad_maximum_fusion), calls=%async_computation | async-start | bytes 524288 | tf_op jit(solution)/shard_map/all_to_all | solution.py:201

commit v2 on v0

v2 whole, which is shorter than its diff:
```python
import jax
import jax.numpy as jnp
from jax import lax
from jax.experimental import pallas as pl
from jax.experimental.pallas import tpu as pltpu
from jax.sharding import PartitionSpec as P


UNROLL = 4
TILE = 256
LINE = 8
TAIL_TILES = 3


def build_weights(weights, ref, base):
    _, blocks, size, width = ref.shape

    def build(i, carry):
        real = ref[0, i]
        imag = ref[1, i]
        weights[base + i, :size, :width] = real
        weights[base + i, :size, width:] = imag
        weights[base + i, size:, :width] = -imag
        weights[base + i, size:, width:] = real
        return carry

    lax.fori_loop(0, blocks, build, 0)


def add_slots(acc, dip_ref, weights, list_ref, count):
    slots = dip_ref.shape[1]
    n_weights = weights.shape[0]

    def group(g, carry):
        for u in range(UNROLL):
            code = list_ref[g * UNROLL + u]
            slot = code // n_weights
            row = slot // slots
            at = code % n_weights
            lhs = jnp.concatenate([dip_ref[row, slot % slots, 0], dip_ref[row, slot % slots, 1]], axis=1)
            acc[row] += jnp.dot(lhs, weights[at], preferred_element_type=jnp.float32)
        return carry

    lax.fori_loop(0, count // UNROLL, group, 0)

    def one(i, carry):
        code = list_ref[i]
        slot = code // n_weights
        row = slot // slots
        at = code % n_weights
        lhs = jnp.concatenate([dip_ref[row, slot % slots, 0], dip_ref[row, slot % slots, 1]], axis=1)
        acc[row] += jnp.dot(lhs, weights[at], preferred_element_type=jnp.float32)
        return carry

    lax.fori_loop(count // UNROLL * UNROLL, count, one, 0)


def own_kernel(
    cols_ref, counts_ref, own_ref, dip_ref, acc_ref, low_list, low_count, high_list, high_count, weights, own_list
):
    rows, slots = dip_ref.shape[:2]
    blocks = own_ref.shape[1]
    build_weights(weights, own_ref, 0)
    acc_ref[...] = jnp.zeros_like(acc_ref)

    def by_row(row, carry):
        def by_slot(j, carry):
            n_low, n_own, n_high = carry
            col = cols_ref[row, j]
            slot = row * slots + j
            is_low = col < blocks
            is_high = col >= 2 * blocks
            is_own = jnp.logical_not(is_low | is_high)

            @pl.when(is_low)
            def _():
                low_list[n_low] = slot * blocks + col

            @pl.when(is_own)
            def _():
                own_list[n_own] = slot * blocks + col - blocks

            @pl.when(is_high)
            def _():
                high_list[n_high] = slot * blocks + col - 2 * blocks

            one = lambda x: x.astype(jnp.int32)
            return n_low + one(is_low), n_own + one(is_own), n_high + one(is_high)

        return lax.fori_loop(0, counts_ref[row], by_slot, carry)

    n_low, n_own, n_high = lax.fori_loop(0, rows, by_row, (jnp.int32(0),) * 3)
    low_count[0] = n_low
    high_count[0] = n_high
    add_slots(acc_ref, dip_ref, weights, own_list, n_own)


def side_kernel(list_ref, count_ref, side_ref, dip_ref, acc_in_ref, out_ref, weights, *scratch):
    build_weights(weights, side_ref, 0)
    acc = scratch[0] if scratch else out_ref
    acc[...] = acc_in_ref[...]
    add_slots(acc, dip_ref, weights, list_ref, count_ref[0])
    if scratch:
        out_ref[...] = acc[...].astype(out_ref.dtype)


def own_products(cols, counts, own, dips):
    rows, slots, _, size, _ = dips.shape
    width = own.shape[-1]
    smem = pl.BlockSpec(memory_space=pltpu.SMEM)
    vmem = pl.BlockSpec(memory_space=pltpu.VMEM)
    slot_list = jax.ShapeDtypeStruct((rows * slots,), jnp.int32)
    one = jax.ShapeDtypeStruct((1,), jnp.int32)
    return pl.pallas_call(
        own_kernel,
        out_shape=(jax.ShapeDtypeStruct((rows, size, 2 * width), jnp.float32), slot_list, one, slot_list, one),
        in_specs=[smem, smem, vmem, vmem],
        out_specs=(vmem, smem, smem, smem, smem),
        scratch_shapes=[
            pltpu.VMEM((rows, 2 * size, 2 * width), jnp.bfloat16),
            pltpu.SMEM((rows * slots,), jnp.int32),
        ],
        compiler_params=pltpu.CompilerParams(vmem_limit_bytes=16 * 1024 * 1024),
        cost_estimate=pl.CostEstimate(flops=1_000_000_000, bytes_accessed=11_000_000, transcendentals=0),
    )(cols, counts, own, dips)


def side_products(slot_list, count, side, dips, acc_in, last):
    rows, _, _, size, _ = dips.shape
    width = side.shape[-1]
    smem = pl.BlockSpec(memory_space=pltpu.SMEM)
    vmem = pl.BlockSpec(memory_space=pltpu.VMEM)
    shape = (rows, size, 2 * width)
    scratch = [pltpu.VMEM((rows, 2 * size, 2 * width), jnp.bfloat16)]
    if last:
        scratch.append(pltpu.VMEM(shape, jnp.float32))
    return pl.pallas_call(
        side_kernel,
        out_shape=jax.ShapeDtypeStruct(shape, jnp.bfloat16 if last else jnp.float32),
        in_specs=[smem, smem, vmem, vmem, vmem],
        out_specs=vmem,
        scratch_shapes=scratch,
        compiler_params=pltpu.CompilerParams(vmem_limit_bytes=16 * 1024 * 1024),
        cost_estimate=pl.CostEstimate(flops=500_000_000, bytes_accessed=12_000_000, transcendentals=0),
    )(slot_list, count, side, dips, acc_in)


def add_tiles(total, left_of, image_ref, other_ref, first, count):
    def tile(i, carry):
        mine = pl.ds(pl.multiple_of(i * TILE, TILE), TILE)
        at = pl.ds(pl.multiple_of((first + i) * TILE, TILE), TILE)
        images = jnp.concatenate([image_ref[at, :], other_ref[at, :]], axis=1)
        for part in range(2):
            total[part] += lax.dot_general(
                left_of(part, mine), images, (((0,), (0,)), ((), ())), preferred_element_type=jnp.float32
            )
        return carry

    lax.fori_loop(0, count, tile, 0)


def combine(mixed, total, width):
    chunks, each2, _ = mixed.shape
    each = each2 // 2
    for t in range(2):
        re = slice(2 * t * width, (2 * t + 1) * width)
        im = slice((2 * t + 1) * width, (2 * t + 2) * width)
        to = slice(t * width, (t + 1) * width)
        real = total[0, :, re] + total[1, :, im]
        imag = total[0, :, im] - total[1, :, re]
        mixed[:, :each, to] = real.reshape(chunks, each, width)
        mixed[:, each:, to] = imag.reshape(chunks, each, width)


def near_kernel(left_ref, image_ref, other_ref, out_ref, total):
    total[...] = jnp.zeros_like(total)
    add_tiles(total, lambda p, at: left_ref[p, at, :], image_ref, other_ref, 0, left_ref.shape[1] // TILE)
    combine(out_ref, total, left_ref.shape[-1])


def tail_kernel(tail0_ref, tail1_ref, image_ref, other_ref, total):
    total[...] = jnp.zeros_like(total)
    first = image_ref.shape[0] // TILE - TAIL_TILES
    tail = lambda p, at: tail0_ref[p, at, :] + tail1_ref[p, at, :]
    add_tiles(total, tail, image_ref, other_ref, first, TAIL_TILES)


def far_kernel(left_ref, image_ref, other_ref, tail_ref, near_ref, out_ref, total, mixed):
    total[...] = tail_ref[...]
    add_tiles(total, lambda p, at: left_ref[p, at, :], image_ref, other_ref, 0, left_ref.shape[1] // TILE)
    combine(mixed, total, left_ref.shape[-1])
    out_ref[...] = jnp.concatenate([near_ref[...], mixed[...]], axis=1).astype(out_ref.dtype)


def project(kernel, out, scratch, *args):
    vmem = pl.BlockSpec(memory_space=pltpu.VMEM)
    return pl.pallas_call(
        kernel,
        out_shape=out,
        in_specs=[vmem] * len(args),
        out_specs=vmem,
        scratch_shapes=[pltpu.VMEM(shape, jnp.float32) for shape in scratch],
        compiler_params=pltpu.CompilerParams(vmem_limit_bytes=12 * 1024 * 1024),
        cost_estimate=pl.CostEstimate(flops=500_000_000, bytes_accessed=3_500_000, transcendentals=0),
    )(*args)


def local(right_vecs, left_vecs, dip_blocks, block_cols, block_counts):
    parts, span, width = right_vecs.shape
    blocks, _, _, size, _ = dip_blocks.shape
    n_rows = lax.axis_size("rows")
    n_cols = lax.axis_size("cols")
    each = width // n_rows
    forward = [(i, i + 1) for i in range(n_rows - 1)]
    backward = [(j, i) for i, j in forward]
    blocked = lambda x: x.reshape(parts, blocks, size, width)
    local_cols = block_cols - (lax.axis_index("rows") - 1) * blocks
    low = lax.ppermute(right_vecs, "rows", forward)
    high = lax.ppermute(right_vecs, "rows", backward)
    split = span - TAIL_TILES * TILE
    main, tail = left_vecs[:, :split], left_vecs[:, split:]
    inner = [(r, 0 < r % LINE < LINE - 1) for r in range(n_rows)]
    out_of = {r: r + 1 if r % LINE == 0 else r - 1 for r, inside in inner if not inside}
    flat = lambda rows: [(r * n_cols + c, r * n_cols + (c ^ 2)) for r in rows for c in range(n_cols)]
    moved = lax.ppermute(tail, "rows", list(out_of.items()))
    moved = lax.ppermute(moved, ("rows", "cols"), flat(out_of.values()))
    across = lax.ppermute(main, "cols", [(i, i ^ 2) for i in range(n_cols)])
    tail_own = lax.ppermute(tail, ("rows", "cols"), flat([r for r, inside in inner if inside]))
    tail_back = lax.ppermute(moved, "rows", [(j, i) for i, j in out_of.items()])
    acc, low_list, low_count, high_list, high_count = own_products(
        local_cols, block_counts, blocked(right_vecs), dip_blocks
    )
    acc = side_products(high_list, high_count, blocked(high), dip_blocks, acc, False)
    image = side_products(low_list, low_count, blocked(low), dip_blocks, acc, True)
    image = image.reshape(span, 2 * width)
    other = lax.ppermute(image, "cols", [(i, i ^ 1) for i in range(n_cols)])
    half = (n_rows, 2 * each, 2 * width)
    products = (2, width, 4 * width)
    near = project(near_kernel, jax.ShapeDtypeStruct(half, jnp.float32), [products], left_vecs, image, other)
    tail_sum = project(tail_kernel, jax.ShapeDtypeStruct(products, jnp.float32), [], tail_own, tail_back, image, other)
    partial = project(
        far_kernel,
        jax.ShapeDtypeStruct((n_rows, 4 * each, 2 * width), jnp.bfloat16),
        [products, half],
        across,
        image,
        other,
        tail_sum,
        near,
    )
    me = lax.axis_index("cols")
    partial, swap_left, swap_right = lax.optimization_barrier((partial, (me & 2) > 0, (me & 1) > 0))
    received = lax.all_to_all(partial, "rows", 0, 0, tiled=True)
    share = jnp.sum(received.astype(jnp.float32), axis=0)
    share = share.reshape(2, parts, each, 2, width)
    share = jnp.where(swap_left, share[::-1], share)
    share = jnp.where(swap_right, share[:, :, :, ::-1], share)
    out = lax.all_gather(share.reshape(2 * parts * each, 2 * width), "cols", axis=0)
    out = out.reshape(2, 2, 2, parts, each, 2, width)
    return out.transpose(2, 1, 4, 3, 0, 5, 6).reshape(n_cols, each, parts, n_cols * width)


def solution(mesh):
    in_specs = (
        P(None, "rows", "cols"),
        P(None, "rows", "cols"),
        P("rows", None, None, None, None),
        P("rows", None),
        P("rows"),
    )
    out_specs = P(None, "rows", None, None)
    return jax.shard_map(local, mesh=mesh, in_specs=in_specs, out_specs=out_specs, check_vma=False)
```

time: 744 us -> 112 us (0.15)
  waiting for transfers between devices: 629 us -> 15.6 us
  starting transfers between devices: 5.93 us -> 23.6 us
  Pallas kernels: 0 us -> 14.5 us
  between operations: 14.2 us -> 0.18 us
  local copies, waits for them, and re-layouts: 21.6 us -> 9.43 us
  matrix products: 9.72 us -> 0 us
  other arithmetic: 9.46 us -> 0.09 us
    unnamed x3 -> x0, waiting for transfers between devices: 561 us -> none
    all_gather x1 -> x0, waiting for transfers between devices: 45.6 us -> none  [local(): lax.all_gather(image, 'cols', axis=2, tiled=True)]
    all_gather x1, blocking collectives: 53.2 us -> 9.67 us  [local(): lax.all_gather(share.reshape(2 * parts * each, 2 * width), 'cols', axis=0)]
    all_to_all x0 -> x1, blocking collectives: none -> 38.6 us  [local(): received = lax.all_to_all(partial, 'rows', 0, 0, tiled=True)]
    ppermute x2 -> x8, starting transfers between devices: 5.71 us -> 23.6 us  [the longest x1 5.16 us: local(): other = lax.ppermute(image, 'cols', [(i, i ^ 1) for i in range(n_cols)])]
    gather x2 -> x0, local copies, waits for them, and re-layouts: 17.1 us -> none  [local(): jnp.take(stacked, local_cols.reshape(-1), axis=1)]
    pallas_call x0 -> x6, Pallas kernels: none -> 14.5 us  [the longest x3 6.58 us: project(): pl.pallas_call(kernel, out_shape=out, in_specs=[vmem] * len(args), out_sp...]
    dot_general x8 -> x0, matrix products: 9.72 us -> none  [the longest x4 5 us: apply_blocks(): jnp.einsum('ijpq,ijqk->ipk', mats, vecs, preferred_element_type=jnp.float32)]
  transfers between devices with their start and end apart: 4 -> 8, of which waited for: 4 -> 3; matrix products, arithmetic and copies ran while one was open for 0% -> 3% of each run, Pallas kernels for 0% -> 11%
where the time goes in v2:
time: 112 us
  blocking collectives  48.2 us (43%)
  starting transfers between devices  23.6 us (21%)
  waiting for transfers between devices  15.6 us (14%)
  Pallas kernels  14.5 us (13%)
  local copies, waits for them, and re-layouts  9.43 us (8%)
    all_to_all x1, blocking collectives, local(): received = lax.all_to_all(partial, 'rows', 0, 0, tiled=True)  38.6 us
    ppermute x1, waiting for transfers between devices, local(): tail_back = lax.ppermute(moved, 'rows', [(j, i) for i, j in out_of.items()])  12 us
    all_gather x1, blocking collectives, local(): lax.all_gather(share.reshape(2 * parts * each, 2 * width), 'cols', axis=0)  9.67 us
    pallas_call x3, Pallas kernels, project(): pl.pallas_call(kernel, out_shape=out, in_specs=[vmem] * len(args), out_sp...  6.58 us
    unnamed x11, local copies, waits for them, and re-layouts  6.03 us
    ppermute x1, starting transfers between devices, local(): other = lax.ppermute(image, 'cols', [(i, i ^ 1) for i in range(n_cols)])  5.16 us
    ppermute x1, starting transfers between devices, local(): low = lax.ppermute(right_vecs, 'rows', forward)  5.06 us
    ppermute x1, starting transfers between devices, local(): across = lax.ppermute(main, 'cols', [(i, i ^ 2) for i in range(n_cols)])  4.45 us
  transfers between devices with their start and end apart: 8, of which 3 were waited for; matrix products, arithmetic and copies ran while one was open for 3% of the time, Pallas kernels for 11%

profile of v2, /device:TPU:1, one launch (start us, length us, event | category | flops | bytes accessed | tf_op | source)
XLA Modules:
  0.0 111.5 jit_solution(5590389691445360830)
XLA Ops:
  0.0 1.3 %collective-permute-start.2 = (bf16[2,2048,128]{2,1,0:T(8,128)(2,1)}, bf16[2,2048,128]{2,1,0:T(8,128)(2,1)S(1)}, u32[]{:S(2)}, u32[]{:S(2)}) collective-permute-start(bf16[2,2048,128]{2,1,0:T(8,128)(2,1)} %param.5), channel_id=1, source_target_pairs={{4,0},{8,4},{12,8},{16,12},{20,16},{24,20},{28,24},{32,28},{36,32}... | collective-permute-start | bytes 3145736 | tf_op jit(solution)/shard_map/ppermute | solution.py:219
  1.3 5.1 %collective-permute-start.1 = (bf16[2,2048,128]{2,1,0:T(8,128)(2,1)}, bf16[2,2048,128]{2,1,0:T(8,128)(2,1)S(1)}, u32[]{:S(2)}, u32[]{:S(2)}) collective-permute-start(bf16[2,2048,128]{2,1,0:T(8,128)(2,1)} %param.5), channel_id=1, source_target_pairs={{0,4},{4,8},{8,12},{12,16},{16,20},{20,24},{24,28},{28,32},{32,36}... | collective-permute-start | bytes 3145736 | tf_op jit(solution)/shard_map/ppermute | solution.py:218
  6.4 1.8 %slice.7 = bf16[2,768,128]{2,1,0:T(8,128)(2,1)} slice(bf16[2,2048,128]{2,1,0:T(8,128)(2,1)} %left_ref.1), slice={[0:2], [1280:2048], [0:128]} | slice | bytes 786432 | tf_op jit(solution)/shard_map/slice | solution.py:221
  8.1 4.2 %collective-permute-start.5 = (bf16[2,768,128]{2,1,0:T(8,128)(2,1)}, bf16[2,768,128]{2,1,0:T(8,128)(2,1)}, u32[]{:S(2)}, u32[]{:S(2)}) collective-permute-start(bf16[2,768,128]{2,1,0:T(8,128)(2,1)} %slice.7), channel_id=1, source_target_pairs={{0,4},{28,24},{32,36},{60,56},{64,68},{92,88},{96,100},{124,120},{... | collective-permute-start | bytes 1179656 | tf_op jit(solution)/shard_map/ppermute | solution.py:225
  12.4 0.8 copy.12
  13.1 3.4 %copy-done = bf16[16,8,2,128,128]{4,3,2,1,0:T(8,128)(2,1)S(1)} copy-done((bf16[16,8,2,128,128]{4,3,2,1,0:T(8,128)(2,1)S(1)}, bf16[16,8,2,128,128]{4,3,2,1,0:T(8,128)(2,1)}, u32[]{:S(2)}) %copy-start) | copy-done | bytes 8388632
  16.5 1.2 %copy-done.3 = bf16[2,2048,128]{2,1,0:T(8,128)(2,1)S(1)} copy-done((bf16[2,2048,128]{2,1,0:T(8,128)(2,1)S(1)}, bf16[2,2048,128]{2,1,0:T(8,128)(2,1)}, u32[]{:S(2)}) %copy-start.3) | copy-done | bytes 1048600
  18.4 3.9 %shard_map.55 = (f32[16,128,256]{2,1,0:T(8,128)S(1)}, s32[128]{0:T(128)S(1)}, s32[1]{0:T(128)}, s32[128]{0:T(128)S(1)}, s32[1]{0:T(128)}) custom-call(s32[16,8]{1,0:T(8,128)S(1)} %broadcast_subtract_fusion.cols_ref, s32[16]{0:T(128)S(1)} %copy-done.4, bf16[2,16,128,128]{3,2,1,0:T(8,128)(2,1)S(1)} %bitcast.10, bf16[16,8,2,128,128]{4,3,2,1,0:T(8,128)(2,1)S(1)} %copy-done), custom_call_target="tpu_custom_call" | custom-call | flops 1000000000 | bytes 11000000 | tf_op jit(solution)/shard_map/pallas_call | solution.py:114
  22.3 3.4 %collective-permute-done.2 = bf16[2,2048,128]{2,1,0:T(8,128)(2,1)S(1)} collective-permute-done((bf16[2,2048,128]{2,1,0:T(8,128)(2,1)}, bf16[2,2048,128]{2,1,0:T(8,128)(2,1)S(1)}, u32[]{:S(2)}, u32[]{:S(2)}) %collective-permute-start.2) | collective-permute-done | bytes 1048608 | tf_op jit(solution)/shard_map/ppermute | solution.py:219
  25.6 2.2 %shard_map.56.acc_in_ref = f32[16,128,256]{2,1,0:T(8,128)S(1)} custom-call(s32[128]{0:T(128)S(1)} %get-tuple-element.15.list_ref, s32[1]{0:T(128)} %get-tuple-element.16.count_ref, bf16[2,16,128,128]{3,2,1,0:T(8,128)(2,1)S(1)} %bitcast.11, bf16[16,8,2,128,128]{4,3,2,1,0:T(8,128)(2,1)S(1)} %copy-done.1, f32[16,128,256]{2,1,0:T(8,128)S(1)} %get-tuple-element.17.acc_in_ref), custom_call_target="tpu_custom_call" | custom-call | flops 500000000 | bytes 12000000 | tf_op jit(solution)/shard_map/pallas_call | solution.py:137
  27.8 1.9 %shard_map.57 = bf16[16,128,256]{2,1,0:T(8,128)(2,1)S(1)} custom-call(s32[128]{0:T(128)S(1)} %get-tuple-element.13.list_ref, s32[1]{0:T(128)} %get-tuple-element.14.count_ref, bf16[2,16,128,128]{3,2,1,0:T(8,128)(2,1)S(1)} %bitcast.9, bf16[16,8,2,128,128]{4,3,2,1,0:T(8,128)(2,1)S(1)} %copy-done.1, f32[16,128,256]{2,1,0:T(8,128)S(1)} %shard_map.56.acc_in_ref), custom_call_target="tpu_custom_call" | custom-call | flops 500000000 | bytes 12000000 | tf_op jit(solution)/shard_map/pallas_call | solution.py:137
  29.7 5.2 %collective-permute-start.3 = (bf16[2048,256]{1,0:T(8,128)(2,1)S(1)}, bf16[2048,256]{1,0:T(8,128)(2,1)S(1)}, u32[]{:S(2)}, u32[]{:S(2)}) collective-permute-start(bf16[2048,256]{1,0:T(8,128)(2,1)S(1)} %bitcast.5), channel_id=1, source_target_pairs={{0,1},{1,0},{2,3},{3,2},{4,5},{5,4},{6,7},{7,6},{8,9},{9,8},{10,11... | collective-permute-start | bytes 3145736 | tf_op jit(solution)/shard_map/ppermute | solution.py:236
  35.1 1.4 %collective-permute-start.6 = (bf16[2,768,128]{2,1,0:T(8,128)(2,1)}, bf16[2,768,128]{2,1,0:T(8,128)(2,1)}, u32[]{:S(2)}, u32[]{:S(2)}) collective-permute-start(bf16[2,768,128]{2,1,0:T(8,128)(2,1)} %collective-permute-done.5), channel_id=1, source_target_pairs={{4,6},{5,7},{6,4},{7,5},{24,26},{25,27},{26,24},{27,25},{36,38},{3... | collective-permute-start | bytes 1179656 | tf_op jit(solution)/shard_map/ppermute | solution.py:226
  36.5 0.9 slice.6
  37.4 4.5 %collective-permute-start = (bf16[2,1280,128]{2,1,0:T(8,128)(2,1)}, bf16[2,1280,128]{2,1,0:T(8,128)(2,1)}, u32[]{:S(2)}, u32[]{:S(2)}) collective-permute-start(bf16[2,1280,128]{2,1,0:T(8,128)(2,1)} %slice.6), channel_id=1, source_target_pairs={{0,2},{1,3},{2,0},{3,1},{4,6},{5,7},{6,4},{7,5},{8,10},{9,11},{10,... | collective-permute-start | bytes 1966088 | tf_op jit(solution)/shard_map/ppermute | solution.py:227
  41.8 0.7 collective-permute-start.4
  42.5 1.3 %collective-permute-start.7 = (bf16[2,768,128]{2,1,0:T(8,128)(2,1)}, bf16[2,768,128]{2,1,0:T(8,128)(2,1)}, u32[]{:S(2)}, u32[]{:S(2)}) collective-permute-start(bf16[2,768,128]{2,1,0:T(8,128)(2,1)} %collective-permute-done.6), channel_id=1, source_target_pairs={{4,0},{24,28},{36,32},{56,60},{68,64},{88,92},{100,96},{120,124},{... | collective-permute-start | bytes 1179656 | tf_op jit(solution)/shard_map/ppermute | solution.py:229
  43.8 2.2 %shard_map.59.near_ref = f32[64,4,256]{2,1,0:T(4,128)S(1)} custom-call(bf16[2,2048,128]{2,1,0:T(8,128)(2,1)S(1)} %copy-done.2, bf16[2048,256]{1,0:T(8,128)(2,1)S(1)} %bitcast.6, bf16[2048,256]{1,0:T(8,128)(2,1)S(1)} %collective-permute-done.3.other_ref), custom_call_target="tpu_custom_call" | custom-call | flops 500000000 | bytes 3500000 | tf_op jit(solution)/shard_map/pallas_call | solution.py:197
  46.0 12.0 %collective-permute-done.7.tail1_ref = bf16[2,768,128]{2,1,0:T(8,128)(2,1)} collective-permute-done((bf16[2,768,128]{2,1,0:T(8,128)(2,1)}, bf16[2,768,128]{2,1,0:T(8,128)(2,1)}, u32[]{:S(2)}, u32[]{:S(2)}) %collective-permute-start.7) | collective-permute-done | bytes 393248 | tf_op jit(solution)/shard_map/ppermute | solution.py:229
  58.0 1.8 %shard_map.58.tail_ref = f32[2,128,512]{2,1,0:T(8,128)S(1)} custom-call(bf16[2,768,128]{2,1,0:T(8,128)(2,1)S(1)} %collective-permute-done.4.tail0_ref, bf16[2,768,128]{2,1,0:T(8,128)(2,1)} %collective-permute-done.7.tail1_ref, bf16[2048,256]{1,0:T(8,128)(2,1)S(1)} %bitcast.7, bf16[2048,256]{1,0:T(8,128)(2,1)S(1)} %collective-permute-done.3.other_ref), custom_call_target="tpu_custom_call" | custom-call | flops 500000000 | bytes 3500000 | tf_op jit(solution)/shard_map/pallas_call | solution.py:197
  59.8 2.6 %shard_map.60 = bf16[64,8,256]{2,1,0:T(8,128)(2,1)S(1)} custom-call(bf16[2,1280,128]{2,1,0:T(8,128)(2,1)} %collective-permute-done.left_ref, bf16[2048,256]{1,0:T(8,128)(2,1)S(1)} %bitcast.8, bf16[2048,256]{1,0:T(8,128)(2,1)S(1)} %collective-permute-done.3.other_ref, f32[2,128,512]{2,1,0:T(8,128)S(1)} %shard_map.58.tail_ref, ...), custom_call_target="tpu_custom_call" | custom-call | flops 500000000 | bytes 3500000 | tf_op jit(solution)/shard_map/pallas_call | solution.py:197
  62.4 38.6 %all_to_all.5 = bf16[64,8,256]{2,1,0:T(8,128)(2,1)S(1)} all-to-all(bf16[64,8,256]{2,1,0:T(8,128)(2,1)S(1)} %shard_map.60), channel_id=1, replica_groups=mesh['rows'=64,'cols'=4] {'rows'}, dimensions={0} | all-to-all | bytes 524288 | tf_op jit(solution)/shard_map/all_to_all | solution.py:253
  101.2 9.7 %all_gather.3 = f32[4,8,256]{2,1,0:T(8,128)S(1)} all-gather(f32[1,8,256]{2,1,0:T(8,128)S(1)} %all_gather_reshape.3), channel_id=1, replica_groups=mesh['rows'=64,'cols'=4] {'cols'}, dimensions={0}, use_global_device_ids=true | all-gather | bytes 40960 | tf_op jit(solution)/shard_map/all_gather | solution.py:258
  110.9 0.7 reshape.27
  (23 shorter events, 1.0 us)
Async XLA Ops:
  0.0 25.6 %collective-permute-start.2 = (bf16[2,2048,128]{2,1,0:T(8,128)(2,1)}, bf16[2,2048,128]{2,1,0:T(8,128)(2,1)S(1)}, u32[]{:S(2)}, u32[]{:S(2)}) collective-permute-start(bf16[2,2048,128]{2,1,0:T(8,128)(2,1)} %param.5), channel_id=1, source_target_pairs={{4,0},{8,4},{12,8},{16,12},{20,16},{24,20},{28,24},{32,28},{36,32}... | collective-permute-start | bytes 3145736 | tf_op jit(solution)/shard_map/ppermute | solution.py:219
  1.3 26.5 %collective-permute-start.1 = (bf16[2,2048,128]{2,1,0:T(8,128)(2,1)}, bf16[2,2048,128]{2,1,0:T(8,128)(2,1)S(1)}, u32[]{:S(2)}, u32[]{:S(2)}) collective-permute-start(bf16[2,2048,128]{2,1,0:T(8,128)(2,1)} %param.5), channel_id=1, source_target_pairs={{0,4},{4,8},{8,12},{12,16},{16,20},{20,24},{24,28},{28,32},{32,36}... | collective-permute-start | bytes 3145736 | tf_op jit(solution)/shard_map/ppermute | solution.py:218
  8.1 26.9 %collective-permute-start.5 = (bf16[2,768,128]{2,1,0:T(8,128)(2,1)}, bf16[2,768,128]{2,1,0:T(8,128)(2,1)}, u32[]{:S(2)}, u32[]{:S(2)}) collective-permute-start(bf16[2,768,128]{2,1,0:T(8,128)(2,1)} %slice.7), channel_id=1, source_target_pairs={{0,4},{28,24},{32,36},{60,56},{64,68},{92,88},{96,100},{124,120},{... | collective-permute-start | bytes 1179656 | tf_op jit(solution)/shard_map/ppermute | solution.py:225
  13.1 3.4 %copy-start = (bf16[16,8,2,128,128]{4,3,2,1,0:T(8,128)(2,1)S(1)}, bf16[16,8,2,128,128]{4,3,2,1,0:T(8,128)(2,1)}, u32[]{:S(2)}) copy-start(bf16[16,8,2,128,128]{4,3,2,1,0:T(8,128)(2,1)} %dip_ref.5) | copy-start | bytes 25165828
  16.5 1.2 %copy-start.3 = (bf16[2,2048,128]{2,1,0:T(8,128)(2,1)S(1)}, bf16[2,2048,128]{2,1,0:T(8,128)(2,1)}, u32[]{:S(2)}) copy-start(bf16[2,2048,128]{2,1,0:T(8,128)(2,1)} %param.5) | copy-start | bytes 3145732
  17.7 0.7 copy-start.4
  18.4 7.2 %copy-start.1 = (bf16[16,8,2,128,128]{4,3,2,1,0:T(8,128)(2,1)S(1)}, bf16[16,8,2,128,128]{4,3,2,1,0:T(8,128)(2,1)}, u32[]{:S(2)}) copy-start(bf16[16,8,2,128,128]{4,3,2,1,0:T(8,128)(2,1)} %dip_ref.5) | copy-start | bytes 25165828
  27.8 8.7 %copy-start.2 = (bf16[2,2048,128]{2,1,0:T(8,128)(2,1)S(1)}, bf16[2,2048,128]{2,1,0:T(8,128)(2,1)}, u32[]{:S(2)}) copy-start(bf16[2,2048,128]{2,1,0:T(8,128)(2,1)} %left_ref.1) | copy-start | bytes 3145732
  29.7 14.1 %collective-permute-start.3 = (bf16[2048,256]{1,0:T(8,128)(2,1)S(1)}, bf16[2048,256]{1,0:T(8,128)(2,1)S(1)}, u32[]{:S(2)}, u32[]{:S(2)}) collective-permute-start(bf16[2048,256]{1,0:T(8,128)(2,1)S(1)} %bitcast.5), channel_id=1, source_target_pairs={{0,1},{1,0},{2,3},{3,2},{4,5},{5,4},{6,7},{7,6},{8,9},{9,8},{10,11... | collective-permute-start | bytes 3145736 | tf_op jit(solution)/shard_map/ppermute | solution.py:236
  35.1 7.4 %collective-permute-start.6 = (bf16[2,768,128]{2,1,0:T(8,128)(2,1)}, bf16[2,768,128]{2,1,0:T(8,128)(2,1)}, u32[]{:S(2)}, u32[]{:S(2)}) collective-permute-start(bf16[2,768,128]{2,1,0:T(8,128)(2,1)} %collective-permute-done.5), channel_id=1, source_target_pairs={{4,6},{5,7},{6,4},{7,5},{24,26},{25,27},{26,24},{27,25},{36,38},{3... | collective-permute-start | bytes 1179656 | tf_op jit(solution)/shard_map/ppermute | solution.py:226
  37.4 22.5 %collective-permute-start = (bf16[2,1280,128]{2,1,0:T(8,128)(2,1)}, bf16[2,1280,128]{2,1,0:T(8,128)(2,1)}, u32[]{:S(2)}, u32[]{:S(2)}) collective-permute-start(bf16[2,1280,128]{2,1,0:T(8,128)(2,1)} %slice.6), channel_id=1, source_target_pairs={{0,2},{1,3},{2,0},{3,1},{4,6},{5,7},{6,4},{7,5},{8,10},{9,11},{10,... | collective-permute-start | bytes 1966088 | tf_op jit(solution)/shard_map/ppermute | solution.py:227
  41.8 4.2 %collective-permute-start.4 = (bf16[2,768,128]{2,1,0:T(8,128)(2,1)}, bf16[2,768,128]{2,1,0:T(8,128)(2,1)S(1)}, u32[]{:S(2)}, u32[]{:S(2)}) collective-permute-start(bf16[2,768,128]{2,1,0:T(8,128)(2,1)} %slice.7), channel_id=1, source_target_pairs={{4,6},{5,7},{6,4},{7,5},{8,10},{9,11},{10,8},{11,9},{12,14},{13,15... | collective-permute-start | bytes 1179656 | tf_op jit(solution)/shard_map/ppermute | solution.py:228
  42.5 15.5 %collective-permute-start.7 = (bf16[2,768,128]{2,1,0:T(8,128)(2,1)}, bf16[2,768,128]{2,1,0:T(8,128)(2,1)}, u32[]{:S(2)}, u32[]{:S(2)}) collective-permute-start(bf16[2,768,128]{2,1,0:T(8,128)(2,1)} %collective-permute-done.6), channel_id=1, source_target_pairs={{4,0},{24,28},{36,32},{56,60},{68,64},{88,92},{100,96},{120,124},{... | collective-permute-start | bytes 1179656 | tf_op jit(solution)/shard_map/ppermute | solution.py:229
